TPU v7x, 32 devices: a whole 2x2x4 slice. The times are simulated.
32 devices in a mesh: row: 4 (over z), col: 8 (over y, x, core).
Axes of the slice: x: 2, y: 2, z: 4, core: 2. Of those that a mesh axis runs over, the one named last changes fastest.
Arguments:
- customer_inputs: bfloat16 [32768, 1024], P(('row', 'col')), may hold values from -6 to 6
- candidate_inputs: bfloat16 [32768, 1024], P(('row', 'col')), may hold values from -6 to 6
- affinity_sharpness: bfloat16 [32768], P(('row', 'col')), may hold values from 4 to 40
- correct_candidate_index: int32 [32768], P(('row', 'col')), may hold values from 0 to 4095
- customer_initial_weights: bfloat16 [1024, 512], replicated, may hold values from -0.1875 to 0.1875
- customer_final_weights: bfloat16 [512, 256], replicated, may hold values from -0.25 to 0.25
- candidate_initial_weights: bfloat16 [1024, 512], replicated, may hold values from -0.1875 to 0.1875
- candidate_final_weights: bfloat16 [512, 256], replicated, may hold values from -0.25 to 0.25
Outputs:
- loss: float32 [], replicated
- grad_user_first: float32 [1024, 512], replicated
- grad_user_second: float32 [512, 256], replicated
- grad_item_first: float32 [1024, 512], replicated
- grad_item_second: float32 [512, 256], replicated
Inputs may be any that keep to these rules, and one draw needn't show every extreme that they name: correct_candidate_index[u] indexes the items of u's group in the order of the steps.
All inputs are finite; a program needn't handle non-finite values.
Results may differ from a plain program's by a relative error of at most 0.015.
Values may be sent and summed in bfloat16 or wider, within the bound.
A program may use at most 128 MiB of HBM per device.

v0:
```python
import jax
import jax.numpy as jnp
from jax import lax
from jax.sharding import PartitionSpec as P

EPS = 1e-06


def tower_forward(feats, first, second):
    pre = jnp.dot(feats, first, preferred_element_type=jnp.float32)
    hidden = jax.nn.relu(pre).astype(jnp.bfloat16)
    out = jnp.dot(hidden, second, preferred_element_type=jnp.float32)
    inv = lax.rsqrt(jnp.mean(out * out, axis=-1, keepdims=True) + EPS)
    return ((out * inv).astype(jnp.bfloat16), (pre, hidden, out, inv))


def tower_backward(feats, second, saved, grad_vec):
    pre, hidden, out, inv = saved
    grad = grad_vec.astype(jnp.float32)
    normed = out * inv
    grad_out = (inv * (grad - normed * jnp.mean(grad * normed, axis=-1, keepdims=True))).astype(
        jnp.bfloat16
    )
    grad_second = jnp.dot(hidden.T, grad_out, preferred_element_type=jnp.float32)
    grad_hidden = jnp.dot(grad_out, second.T, preferred_element_type=jnp.float32)
    grad_pre = jnp.where(pre > 0, grad_hidden, 0.0).astype(jnp.bfloat16)
    grad_first = jnp.dot(feats.T, grad_pre, preferred_element_type=jnp.float32)
    return (grad_first, grad_second)


def positive_pair_logit(
    shopper_vector, gathered_entries, affinity_sharpness, correct_candidate_index, resident_table
):
    latent_code = shopper_vector.shape[-1]
    coolness_fp32_number = affinity_sharpness.astype(jnp.float32)
    affinity_matrix = (
        coolness_fp32_number[:, None]
        * jnp.einsum(
            "ue,ie->ui", shopper_vector, gathered_entries, preferred_element_type=jnp.float32
        )
        / latent_code
    )
    lse = jax.nn.logsumexp(affinity_matrix, axis=1)
    columns = lax.broadcasted_iota(jnp.int32, affinity_matrix.shape, 1)
    target_column = columns == correct_candidate_index[:, None]
    picked = jnp.sum(jnp.where(target_column, affinity_matrix, 0.0), axis=1)
    softmax_likelihood = jnp.exp(affinity_matrix - lse[:, None])
    sensitivity_of_affinities = (
        (softmax_likelihood - target_column.astype(jnp.float32))
        * (coolness_fp32_number / (latent_code * resident_table))[:, None]
    ).astype(jnp.bfloat16)
    customer_derivative = jnp.dot(
        sensitivity_of_affinities, gathered_entries, preferred_element_type=jnp.float32
    )
    return (lse, sensitivity_of_affinities, customer_derivative, jnp.sum(lse - picked))


def body(
    customer_inputs,
    candidate_inputs,
    affinity_sharpness,
    correct_candidate_index,
    customer_initial_weights,
    customer_final_weights,
    candidate_initial_weights,
    candidate_final_weights,
):
    resident_table = customer_inputs.shape[0]
    shopper_vector, user_saved = tower_forward(
        customer_inputs, customer_initial_weights, customer_final_weights
    )
    offered_thing_vector, item_saved = tower_forward(
        candidate_inputs, candidate_initial_weights, candidate_final_weights
    )
    latent_code = shopper_vector.shape[-1]
    gathered_entries = lax.all_gather(offered_thing_vector, "row", axis=0, tiled=True)
    lse, sensitivity_of_affinities, customer_derivative, loss_local = positive_pair_logit(
        shopper_vector,
        gathered_entries,
        affinity_sharpness,
        correct_candidate_index,
        resident_table,
    )
    all_users, all_scales = (
        lax.all_gather(shopper_vector, "row", axis=0, tiled=True),
        lax.all_gather(affinity_sharpness, "row", axis=0, tiled=True),
    )
    all_positive = lax.all_gather(correct_candidate_index, "row", axis=0, tiled=True)
    all_lse = lax.all_gather(lse, "row", axis=0, tiled=True)
    coolness_fp32_number = all_scales.astype(jnp.float32)
    affinity_matrix = (
        coolness_fp32_number[:, None]
        * jnp.einsum(
            "ue,ie->ui", all_users, offered_thing_vector, preferred_element_type=jnp.float32
        )
        / latent_code
    )
    start = lax.axis_index("row") * resident_table
    columns = lax.broadcasted_iota(jnp.int32, affinity_matrix.shape, 1) + start
    target_column = columns == all_positive[:, None]
    softmax_likelihood = jnp.exp(affinity_matrix - all_lse[:, None])
    group_dlogits = (
        (softmax_likelihood - target_column.astype(jnp.float32))
        * (coolness_fp32_number / (latent_code * resident_table))[:, None]
    ).astype(jnp.bfloat16)
    candidate_derivative = jnp.einsum(
        "ui,ue->ie", group_dlogits, all_users, preferred_element_type=jnp.float32
    )
    grad_user_first, grad_user_second = tower_backward(
        customer_inputs,
        customer_final_weights,
        user_saved,
        customer_derivative.astype(jnp.bfloat16),
    )
    grad_item_first, grad_item_second = tower_backward(
        candidate_inputs,
        candidate_final_weights,
        item_saved,
        candidate_derivative.astype(jnp.bfloat16),
    )
    summed = lax.psum(
        (grad_user_first, grad_user_second, grad_item_first, grad_item_second, loss_local),
        ("row", "col"),
    )
    users_total = resident_table * lax.axis_size("row") * lax.axis_size("col")
    return (summed[4] / users_total, summed[0], summed[1], summed[2], summed[3])


def solution(mesh):
    placed = (
        P(("row", "col"), None),
        P(("row", "col"), None),
        P(("row", "col")),
        P(("row", "col")),
        P(),
        P(),
        P(),
        P(),
    )
    return jax.shard_map(
        body, mesh=mesh, in_specs=placed, out_specs=(P(), P(), P(), P(), P()), check_vma=False
    )
```

profile of v0, /device:TPU:0, one launch (start us, length us, event | category | flops | bytes accessed | tf_op | source)
XLA Modules:
  0.0 292.9 jit_solution(12754401451739418101)
XLA Ops:
  7.2 3.3 %fusion.26 = f32[1024,512]{1,0:T(8,128)S(1)} fusion(bf16[1024,1024]{1,0:T(8,128)(2,1)} %param.9, bf16[1024,512]{1,0:T(8,128)(2,1)} %param.14), kind=kOutput, calls=%fused_computation.56 | convolution fusion | flops 1073741824 | bytes 5242880 | tf_op jit(solution)/shard_map/dot_general | solution.py:10
  10.5 1.3 copy-done.3
  12.4 0.9 multiply_convert_fusion.5
  13.4 2.5 fusion.25
  15.9 1.3 copy-done.4
  17.7 0.9 copy-done.1
  19.7 14.1 %all_gather.16 = bf16[4096]{0:T(1024)(128)(2,1)S(1)} all-gather(bf16[1024]{0:T(1024)(128)(2,1)S(1)} %copy-done.14), channel_id=1, replica_groups=mesh['row'=4,'col'=8] {'row'}, dimensions={0}, use_global_device_ids=true | all-gather | bytes 10240 | tf_op jit(solution)/shard_map/all_gather | solution.py:86
  33.8 13.6 %all_gather.19 = s32[4096]{0:T(1024)S(1)} all-gather(s32[1024]{0:T(1024)S(1)} %copy-done.15), channel_id=1, replica_groups=mesh['row'=4,'col'=8] {'row'}, dimensions={0}, use_global_device_ids=true | all-gather | bytes 20480 | tf_op jit(solution)/shard_map/all_gather | solution.py:88
  47.4 14.8 %all-gather.3.cloned.1.call-done = bf16[4096,256]{0,1:T(8,128)(2,1)} async-done(((bf16[1024,256]{0,1:T(8,128)(2,1)}), bf16[4096,256]{0,1:T(8,128)(2,1)}) %all-gather.3.cloned.1.call-update) | async-done | bytes 2097168 | tf_op jit(solution)/shard_map/all_gather | solution.py:76
  62.2 4.3 %fusion = (f32[1024]{0:T(1024)S(1)}, f32[1024,4096]{1,0:T(8,128)S(1)}) fusion(f32[1024]{0:T(1024)S(1)} %convert_element_type.54, bf16[1024,256]{0,1:T(8,128)(2,1)} %multiply_convert_fusion.6, bf16[4096,256]{0,1:T(8,128)(2,1)} %all-gather.3.cloned.1.call-done), kind=kOutput, calls=%fused_computation.6 | convolution fusion | flops 2160065536 | bytes 19406848 | tf_op jit(solution)/shard_map/ue,ie->ui/dot_general | solution.py:38
  66.5 6.9 %select_reduce_fusion = (f32[1024]{0:T(1024)S(1)}, f32[1024]{0:T(1024)S(1)}) fusion(f32[1024,4096]{1,0:T(8,128)S(1)} %get-tuple-element.28, s32[1024]{0:T(1024)S(1)} %copy-done.15, f32[1024]{0:T(1024)S(1)} %convert_element_type.54, f32[1024]{0:T(1024)S(1)} %is-finite_select_fusion), kind=kLoop, calls=%fused_computation.2 | loop fusion | flops 29358080 | bytes 16797696 | tf_op jit(solution)/shard_map/reduce_sum | solution.py:46
  74.0 13.8 %all_gather.18 = f32[4096]{0:T(1024)S(1)} all-gather(f32[1024]{0:T(1024)S(1)} %get-tuple-element.22), channel_id=1, replica_groups=mesh['row'=4,'col'=8] {'row'}, dimensions={0}, use_global_device_ids=true | all-gather | bytes 20480 | tf_op jit(solution)/shard_map/all_gather | solution.py:89
  87.8 7.9 %fusion.5 = (f32[1024]{0:T(1024)S(1)}, bf16[1024,256]{0,1:T(8,128)(2,1)S(1)}) fusion(f32[1024,256]{0,1:T(8,128)S(1)} %copy-done.2, f32[1024]{0:T(1024)S(1)} %add_rsqrt_fusion.1, bf16[4096,256]{0,1:T(8,128)(2,1)S(1)} %copy-done.6, f32[1024,4096]{1,0:T(8,128)S(1)} %get-tuple-element.28, f32[1024]{0:T(1024)S(1)} %broadcast_multiply_fusion.1, ...), kind=kOutput, calls=%fused_computation.21 | convolution fusion | flops 2182347776 | bytes 20471808 | tf_op jit(solution)/shard_map/dot_general | solution.py:52
  97.5 1.3 fusion.13
  98.8 4.7 %convolution_bitcast_fusion.1 = f32[1024,512]{0,1:T(8,128)} fusion(bf16[1024,1024]{1,0:T(8,128)(2,1)S(1)} %copy-done, f32[1024,512]{1,0:T(8,128)} %copy-done.4, bf16[1024,256]{0,1:T(8,128)(2,1)} %copy-done.7, bf16[512,256]{1,0:T(8,128)(2,1)S(1)} %copy-done.11), kind=kOutput, calls=%fused_computation.14 | convolution fusion | flops 1343750144 | bytes 7077888 | tf_op jit(solution)/shard_map/dot_general | solution.py:27
  103.5 5.5 %all-gather.5.cloned.1.call-done = bf16[4096,256]{0,1:T(8,128)(2,1)} async-done(((bf16[1024,256]{0,1:T(8,128)(2,1)}), bf16[4096,256]{0,1:T(8,128)(2,1)}) %all-gather.5.cloned.1.call-update) | async-done | bytes 2097168 | tf_op jit(solution)/shard_map/all_gather | solution.py:85
  109.1 10.3 %fusion.8 = (f32[1024]{0:T(1024)S(1)}, bf16[1024,256]{0,1:T(8,128)(2,1)}) fusion(f32[1024,256]{0,1:T(8,128)S(1)} %get-tuple-element.26, f32[1024]{0:T(1024)S(1)} %add_rsqrt_fusion, bf16[4096,256]{0,1:T(8,128)(2,1)} %all-gather.5.cloned.1.call-done, f32[4096]{0:T(1024)S(1)} %broadcast_multiply_fusion, s32[1024]{0:T(1024)S(1)} %iota_add_fusion, ...), kind=kOutput, calls=%fused_computation.24 | convolution fusion | flops 4330355712 | bytes 3747840 | tf_op jit(solution)/shard_map/ui,ue->ie/dot_general | solution.py:106
  119.4 2.1 fusion.10
  121.4 5.4 %convolution_bitcast_fusion = f32[1024,512]{0,1:T(8,128)} fusion(bf16[1024,1024]{1,0:T(8,128)(2,1)} %param.9, f32[1024,512]{1,0:T(8,128)} %copy-done.3, bf16[1024,256]{0,1:T(8,128)(2,1)} %fusion.10, bf16[512,256]{1,0:T(8,128)(2,1)S(1)} %copy-done.13), kind=kOutput, calls=%fused_computation.13 | convolution fusion | flops 1343750144 | bytes 7077888 | tf_op jit(solution)/shard_map/dot_general | solution.py:27
  126.8 2.9 fusion.15
  129.7 39.7 %psum.35 = f32[]{:T(128)} all-reduce(f32[]{:T(128)} %get-tuple-element.21), channel_id=1, replica_groups=mesh['row'=4,'col'=8] {'row','col'}, use_global_device_ids=true, to_apply=%region_6.7 | all-reduce | flops 1 | bytes 8 | tf_op jit(solution)/shard_map/psum | solution.py:121
  170.0 107.8 %all-reduce.3.cloned.1.call-done = (f32[1024,512]{0,1:T(8,128)}, f32[512,256]{1,0:T(8,128)}, f32[1024,512]{0,1:T(8,128)}, f32[512,256]{1,0:T(8,128)}) async-done(((f32[1024,512]{0,1:T(8,128)}, f32[512,256]{1,0:T(8,128)}, f32[1024,512]{0,1:T(8,128)}, f32[512,256]{1,0:T(8,128)}), (f32[1024,512]{0,1:T(8,128)}, f32[512,256]{1,0:T(8,128)}, f32[1024,512]{0,1:T(8,128)}, ...) | async-done | bytes 5242896 | tf_op jit(solution)/shard_map/psum | solution.py:121
  277.8 2.9 copy.15
  280.7 3.0 %copy.16 = f32[1024,512]{1,0:T(8,128)} copy(f32[1024,512]{0,1:T(8,128)} %get-tuple-element.19) | data formatting | bytes 4194304
  (52 shorter events, 6.1 us)
Async XLA Ops:
  7.2 6.2 %copy-start = (bf16[1024,1024]{1,0:T(8,128)(2,1)S(1)}, bf16[1024,1024]{1,0:T(8,128)(2,1)}, u32[]{:S(2)}) copy-start(bf16[1024,1024]{1,0:T(8,128)(2,1)} %param.8) | copy-start | bytes 6291460
  7.2 4.7 %copy-start.12 = (bf16[512,256]{1,0:T(8,128)(2,1)S(1)}, bf16[512,256]{1,0:T(8,128)(2,1)}, u32[]{:S(2)}) copy-start(bf16[512,256]{1,0:T(8,128)(2,1)} %param.15) | copy-start | bytes 786436
  7.2 55.0 %all-gather.3.cloned.1.call-start = ((), (), s32[]{:S(2)}) async-start(), calls=%async_computation | async-start | bytes 2621440 | tf_op jit(solution)/shard_map/all_gather | solution.py:76
  10.5 1.3 copy-start.3
  13.3 3.9 %copy-start.11 = (bf16[512,256]{1,0:T(8,128)(2,1)S(1)}, bf16[512,256]{1,0:T(8,128)(2,1)}, u32[]{:S(2)}) copy-start(bf16[512,256]{1,0:T(8,128)(2,1)} %param.13) | copy-start | bytes 786436
  13.3 95.8 %all-gather.5.cloned.1.call-start = ((), (), s32[]{:S(2)}) async-start(), calls=%async_computation.1 | async-start | bytes 2621440 | tf_op jit(solution)/shard_map/all_gather | solution.py:85
  15.9 1.3 copy-start.4
  17.2 2.4 copy-start.14
  17.2 16.6 %copy-start.15 = (s32[1024]{0:T(1024)S(1)}, s32[1024]{0:T(1024)}, u32[]{:S(2)}) copy-start(s32[1024]{0:T(1024)} %param.11) | copy-start | bytes 12292
  17.7 1.0 copy-start.1
  19.6 258.2 %all-reduce.3.cloned.1.call-start = ((), (), s32[]{:S(2)}) async-start(), calls=%async_computation.2 | async-start | bytes 10485760 | tf_op jit(solution)/shard_map/psum | solution.py:121
  66.4 21.3 %copy-start.2 = (f32[1024,256]{0,1:T(8,128)S(1)}, f32[1024,256]{0,1:T(8,128)}, u32[]{:S(2)}) copy-start(f32[1024,256]{0,1:T(8,128)} %copy-done.1) | copy-start | bytes 3145732
  66.4 21.3 %copy-start.6 = (bf16[4096,256]{0,1:T(8,128)(2,1)S(1)}, bf16[4096,256]{0,1:T(8,128)(2,1)}, u32[]{:S(2)}) copy-start(bf16[4096,256]{0,1:T(8,128)(2,1)} %all-gather.3.cloned.1.call-done) | copy-start | bytes 6291460
  95.7 1.8 copy-start.5
  95.9 0.8 copy-start.7
  119.3 2.1 copy-start.13
  121.4 5.4 %copy-start.8 = (bf16[1024,256]{0,1:T(8,128)(2,1)S(1)}, bf16[1024,256]{0,1:T(8,128)(2,1)}, u32[]{:S(2)}) copy-start(bf16[1024,256]{0,1:T(8,128)(2,1)} %fusion.10) | copy-start | bytes 1572868
  280.7 3.0 %copy-start.10 = (f32[512,256]{1,0:T(8,128)S(1)}, f32[512,256]{1,0:T(8,128)}, u32[]{:S(2)}) copy-start(f32[512,256]{1,0:T(8,128)} %get-tuple-element.35) | copy-start | bytes 1572868
  280.7 3.8 %copy-start.9 = (f32[512,256]{1,0:T(8,128)S(1)}, f32[512,256]{1,0:T(8,128)}, u32[]{:S(2)}) copy-start(f32[512,256]{1,0:T(8,128)} %get-tuple-element.37) | copy-start | bytes 1572868
Sparse Core Ops, SparseCore 0:
  13.4 48.7 all-gather.2
  64.3 44.7 all-gather.4
  129.8 147.9 all-reduce.2
where the time goes:
time: 293 us
  waiting for transfers between devices  128 us (44%)
  blocking collectives  81.1 us (28%)
  matrix products  43.5 us (15%)
  between operations  15.7 us (5%)
  local copies, waits for them, and re-layouts  12.6 us (4%)
  other arithmetic  11.6 us (4%)
    psum x1, waiting for transfers between devices, body(): lax.psum((grad_user_first, grad_user_second, grad_item_first, grad_item_s...  108 us
    psum x1, blocking collectives, body(): lax.psum((grad_user_first, grad_user_second, grad_item_first, grad_item_s...  39.7 us
    all_gather x1, waiting for transfers between devices, body(): lax.all_gather(offered_thing_vector, 'row', axis=0, tiled=True)  14.8 us
    all_gather x1, blocking collectives, body(): lax.all_gather(affinity_sharpness, 'row', axis=0, tiled=True)  14.1 us
    all_gather x1, blocking collectives, body(): all_lse = lax.all_gather(lse, 'row', axis=0, tiled=True)  13.8 us
    all_gather x1, blocking collectives, body(): lax.all_gather(correct_candidate_index, 'row', axis=0, tiled=True)  13.6 us
    unnamed x36, local copies, waits for them, and re-layouts  12.6 us
    dot_general x1, matrix products, body(): jnp.einsum('ui,ue->ie', group_dlogits, all_users, preferred_element_type=...  10.3 us
  transfers between devices with their start and end apart: 3, of which 3 were waited for; matrix products, arithmetic and copies ran while one was open for 10% of the time, Pallas kernels for 0%

commit v1 on v0

--- a/solution.py
+++ b/solution.py
@@ -118,9 +118,12 @@
         item_saved,
         candidate_derivative.astype(jnp.bfloat16),
     )
-    summed = lax.psum(
-        (grad_user_first, grad_user_second, grad_item_first, grad_item_second, loss_local),
-        ("row", "col"),
+    summed = jax.lax.psum(
+        jax.lax.psum(
+            (grad_user_first, grad_user_second, grad_item_first, grad_item_second, loss_local),
+            "col",
+        ),
+        "row",
     )
     users_total = resident_table * lax.axis_size("row") * lax.axis_size("col")
     return (summed[4] / users_total, summed[0], summed[1], summed[2], summed[3])

time: 293 us -> 428 us (1.46)
  waiting for transfers between devices: 128 us -> 276 us
  blocking collectives: 81.1 us -> 68.1 us
    psum x1 -> x2, waiting for transfers between devices: 108 us -> 256 us  [the longest x1 164 us: body(): jax.lax.psum(jax.lax.psum((grad_user_first, grad_user_second, grad_item_f...]
    psum x1 -> x2, blocking collectives: 39.7 us -> 26.7 us  [the longest x1 13.4 us: body(): jax.lax.psum((grad_user_first, grad_user_second, grad_item_first, grad_it...]
  transfers between devices with their start and end apart: 3 -> 4, of which waited for: 3 -> 4; matrix products, arithmetic and copies ran while one was open for 10% -> 7% of each run, Pallas kernels for 0% -> 0%
where the time goes in v1:
time: 428 us
  waiting for transfers between devices  276 us (64%)
  blocking collectives  68.1 us (16%)
  matrix products  43.5 us (10%)
  between operations  15.8 us (4%)
  local copies, waits for them, and re-layouts  12.6 us (3%)
  other arithmetic  11.6 us (3%)
    psum x1, waiting for transfers between devices, body(): jax.lax.psum(jax.lax.psum((grad_user_first, grad_user_second, grad_item_f...  164 us
    psum x1, waiting for transfers between devices, body(): jax.lax.psum((grad_user_first, grad_user_second, grad_item_first, grad_it...  91.4 us
    all_gather x1, waiting for transfers between devices, body(): lax.all_gather(offered_thing_vector, 'row', axis=0, tiled=True)  14.9 us
    all_gather x1, blocking collectives, body(): lax.all_gather(affinity_sharpness, 'row', axis=0, tiled=True)  14.1 us
    all_gather x1, blocking collectives, body(): all_lse = lax.all_gather(lse, 'row', axis=0, tiled=True)  13.8 us
    all_gather x1, blocking collectives, body(): lax.all_gather(correct_candidate_index, 'row', axis=0, tiled=True)  13.5 us
    psum x1, blocking collectives, body(): jax.lax.psum((grad_user_first, grad_user_second, grad_item_first, grad_it...  13.4 us
    psum x1, blocking collectives, body(): jax.lax.psum(jax.lax.psum((grad_user_first, grad_user_second, grad_item_f...  13.3 us
  transfers between devices with their start and end apart: 4, of which 4 were waited for; matrix products, arithmetic and copies ran while one was open for 7% of the time, Pallas kernels for 0%

profile of v1, /device:TPU:0, one launch (start us, length us, event | category | flops | bytes accessed | tf_op | source)
XLA Modules:
  0.0 428.0 jit_solution(17085692951126846788)
XLA Ops:
  7.2 3.3 fusion.26
  10.5 1.3 copy-done.3
  13.4 2.5 fusion.25
  15.9 1.3 copy-done.4
  19.7 14.1 %all_gather.16 = bf16[4096]{0:T(1024)(128)(2,1)S(1)} all-gather(bf16[1024]{0:T(1024)(128)(2,1)S(1)} %copy-done.14), channel_id=1, replica_groups=mesh['row'=4,'col'=8] {'row'}, dimensions={0}, use_global_device_ids=true | all-gather | bytes 10240 | tf_op jit(solution)/shard_map/all_gather | solution.py:86
  33.8 13.5 %all_gather.19 = s32[4096]{0:T(1024)S(1)} all-gather(s32[1024]{0:T(1024)S(1)} %copy-done.15), channel_id=1, replica_groups=mesh['row'=4,'col'=8] {'row'}, dimensions={0}, use_global_device_ids=true | all-gather | bytes 20480 | tf_op jit(solution)/shard_map/all_gather | solution.py:88
  47.3 14.9 %all-gather.3.cloned.1.call-done = bf16[4096,256]{0,1:T(8,128)(2,1)} async-done(((bf16[1024,256]{0,1:T(8,128)(2,1)}), bf16[4096,256]{0,1:T(8,128)(2,1)}) %all-gather.3.cloned.1.call-update) | async-done | bytes 2097168 | tf_op jit(solution)/shard_map/all_gather | solution.py:76
  62.2 4.3 fusion
  66.5 6.9 %select_reduce_fusion = (f32[1024]{0:T(1024)S(1)}, f32[1024]{0:T(1024)S(1)}) fusion(f32[1024,4096]{1,0:T(8,128)S(1)} %get-tuple-element.32, s32[1024]{0:T(1024)S(1)} %copy-done.15, f32[1024]{0:T(1024)S(1)} %convert_element_type.54, f32[1024]{0:T(1024)S(1)} %is-finite_select_fusion), kind=kLoop, calls=%fused_computation.2 | loop fusion | flops 29358080 | bytes 16797696 | tf_op jit(solution)/shard_map/reduce_sum | solution.py:46
  74.0 13.8 %all_gather.18 = f32[4096]{0:T(1024)S(1)} all-gather(f32[1024]{0:T(1024)S(1)} %get-tuple-element.26), channel_id=1, replica_groups=mesh['row'=4,'col'=8] {'row'}, dimensions={0}, use_global_device_ids=true | all-gather | bytes 20480 | tf_op jit(solution)/shard_map/all_gather | solution.py:89
  87.8 7.9 %fusion.5 = (f32[1024]{0:T(1024)S(1)}, bf16[1024,256]{0,1:T(8,128)(2,1)S(1)}) fusion(f32[1024,256]{0,1:T(8,128)S(1)} %copy-done.2, f32[1024]{0:T(1024)S(1)} %add_rsqrt_fusion.1, bf16[4096,256]{0,1:T(8,128)(2,1)S(1)} %copy-done.6, f32[1024,4096]{1,0:T(8,128)S(1)} %get-tuple-element.32, f32[1024]{0:T(1024)S(1)} %broadcast_multiply_fusion.1, ...), kind=kOutput, calls=%fused_computation.21 | convolution fusion | flops 2182347776 | bytes 20471808 | tf_op jit(solution)/shard_map/dot_general | solution.py:52
  97.5 1.3 fusion.13
  98.8 4.7 %convolution_bitcast_fusion.1 = f32[1024,512]{0,1:T(8,128)} fusion(bf16[1024,1024]{1,0:T(8,128)(2,1)S(1)} %copy-done, f32[1024,512]{1,0:T(8,128)} %copy-done.4, bf16[1024,256]{0,1:T(8,128)(2,1)} %copy-done.7, bf16[512,256]{1,0:T(8,128)(2,1)S(1)} %copy-done.11), kind=kOutput, calls=%fused_computation.14 | convolution fusion | flops 1343750144 | bytes 7077888 | tf_op jit(solution)/shard_map/dot_general | solution.py:27
  103.5 5.6 %all-gather.5.cloned.1.call-done = bf16[4096,256]{0,1:T(8,128)(2,1)} async-done(((bf16[1024,256]{0,1:T(8,128)(2,1)}), bf16[4096,256]{0,1:T(8,128)(2,1)}) %all-gather.5.cloned.1.call-update) | async-done | bytes 2097168 | tf_op jit(solution)/shard_map/all_gather | solution.py:85
  109.1 10.3 %fusion.8 = (f32[1024]{0:T(1024)S(1)}, bf16[1024,256]{0,1:T(8,128)(2,1)}) fusion(f32[1024,256]{0,1:T(8,128)S(1)} %get-tuple-element.30, f32[1024]{0:T(1024)S(1)} %add_rsqrt_fusion, bf16[4096,256]{0,1:T(8,128)(2,1)} %all-gather.5.cloned.1.call-done, f32[4096]{0:T(1024)S(1)} %broadcast_multiply_fusion, s32[1024]{0:T(1024)S(1)} %iota_add_fusion, ...), kind=kOutput, calls=%fused_computation.24 | convolution fusion | flops 4330355712 | bytes 3747840 | tf_op jit(solution)/shard_map/ui,ue->ie/dot_general | solution.py:106
  119.4 2.1 fusion.10
  121.4 5.4 %convolution_bitcast_fusion = f32[1024,512]{0,1:T(8,128)} fusion(bf16[1024,1024]{1,0:T(8,128)(2,1)} %param.9, f32[1024,512]{1,0:T(8,128)} %copy-done.3, bf16[1024,256]{0,1:T(8,128)(2,1)} %fusion.10, bf16[512,256]{1,0:T(8,128)(2,1)S(1)} %copy-done.13), kind=kOutput, calls=%fused_computation.13 | convolution fusion | flops 1343750144 | bytes 7077888 | tf_op jit(solution)/shard_map/dot_general | solution.py:27
  126.8 2.9 fusion.15
  129.8 91.4 %all-reduce.5.cloned.1.call-done = (f32[1024,512]{0,1:T(8,128)}, f32[512,256]{1,0:T(8,128)}, f32[1024,512]{0,1:T(8,128)}, f32[512,256]{1,0:T(8,128)}) async-done(((f32[1024,512]{0,1:T(8,128)}, f32[512,256]{1,0:T(8,128)}, f32[1024,512]{0,1:T(8,128)}, f32[512,256]{1,0:T(8,128)}), (f32[1024,512]{0,1:T(8,128)}, f32[512,256]{1,0:T(8,128)}, f32[1024,512]{0,1:T(8,128)}, ...) | async-done | bytes 5242896 | tf_op jit(solution)/shard_map/psum | solution.py:122
  221.2 13.4 %psum.70 = f32[]{:T(128)} all-reduce(f32[]{:T(128)} %get-tuple-element.25), channel_id=1, replica_groups=mesh['row'=4,'col'=8] {'col'}, use_global_device_ids=true, to_apply=%region_6.7 | all-reduce | flops 1 | bytes 8 | tf_op jit(solution)/shard_map/psum | solution.py:122
  234.6 13.3 %psum.71 = f32[]{:T(128)} all-reduce(f32[]{:T(128)} %psum.70), channel_id=1, replica_groups=mesh['row'=4,'col'=8] {'row'}, use_global_device_ids=true, to_apply=%region_7.8 | all-reduce | flops 1 | bytes 8 | tf_op jit(solution)/shard_map/psum | solution.py:121
  248.5 164.4 %all-reduce.7.cloned.1.call-done = (f32[1024,512]{0,1:T(8,128)}, f32[512,256]{1,0:T(8,128)}, f32[1024,512]{0,1:T(8,128)}, f32[512,256]{1,0:T(8,128)}) async-done(((f32[1024,512]{0,1:T(8,128)}, f32[512,256]{1,0:T(8,128)}, f32[1024,512]{0,1:T(8,128)}, f32[512,256]{1,0:T(8,128)}), (f32[1024,512]{0,1:T(8,128)}, f32[512,256]{1,0:T(8,128)}, f32[1024,512]{0,1:T(8,128)}, ...) | async-done | bytes 5242896 | tf_op jit(solution)/shard_map/psum | solution.py:121
  412.9 2.9 copy.15
  415.8 3.0 copy.16
  (56 shorter events, 8.0 us)
Async XLA Ops:
  7.2 6.2 %copy-start = (bf16[1024,1024]{1,0:T(8,128)(2,1)S(1)}, bf16[1024,1024]{1,0:T(8,128)(2,1)}, u32[]{:S(2)}) copy-start(bf16[1024,1024]{1,0:T(8,128)(2,1)} %param.8) | copy-start | bytes 6291460
  7.2 4.7 %copy-start.12 = (bf16[512,256]{1,0:T(8,128)(2,1)S(1)}, bf16[512,256]{1,0:T(8,128)(2,1)}, u32[]{:S(2)}) copy-start(bf16[512,256]{1,0:T(8,128)(2,1)} %param.15) | copy-start | bytes 786436
  7.2 55.0 %all-gather.3.cloned.1.call-start = ((), (), s32[]{:S(2)}) async-start(), calls=%async_computation | async-start | bytes 2621440 | tf_op jit(solution)/shard_map/all_gather | solution.py:76
  10.5 1.3 copy-start.3
  13.3 3.9 copy-start.11
  13.3 95.8 %all-gather.5.cloned.1.call-start = ((), (), s32[]{:S(2)}) async-start(), calls=%async_computation.1 | async-start | bytes 2621440 | tf_op jit(solution)/shard_map/all_gather | solution.py:85
  15.9 1.3 copy-start.4
  17.2 2.4 copy-start.14
  17.2 16.6 %copy-start.15 = (s32[1024]{0:T(1024)S(1)}, s32[1024]{0:T(1024)}, u32[]{:S(2)}) copy-start(s32[1024]{0:T(1024)} %param.11) | copy-start | bytes 12292
  17.7 1.0 copy-start.1
  19.6 201.6 %all-reduce.5.cloned.1.call-start = ((), (), s32[]{:S(2)}) async-start(), calls=%async_computation.2 | async-start | bytes 10485760 | tf_op jit(solution)/shard_map/psum | solution.py:122
  66.4 21.3 %copy-start.2 = (f32[1024,256]{0,1:T(8,128)S(1)}, f32[1024,256]{0,1:T(8,128)}, u32[]{:S(2)}) copy-start(f32[1024,256]{0,1:T(8,128)} %copy-done.1) | copy-start | bytes 3145732
  66.4 21.3 %copy-start.6 = (bf16[4096,256]{0,1:T(8,128)(2,1)S(1)}, bf16[4096,256]{0,1:T(8,128)(2,1)}, u32[]{:S(2)}) copy-start(bf16[4096,256]{0,1:T(8,128)(2,1)} %all-gather.3.cloned.1.call-done) | copy-start | bytes 6291460
  95.7 1.8 copy-start.5
  95.9 0.8 copy-start.7
  119.4 2.1 copy-start.13
  121.4 5.4 %copy-start.8 = (bf16[1024,256]{0,1:T(8,128)(2,1)S(1)}, bf16[1024,256]{0,1:T(8,128)(2,1)}, u32[]{:S(2)}) copy-start(bf16[1024,256]{0,1:T(8,128)(2,1)} %fusion.10) | copy-start | bytes 1572868
  129.7 283.2 %all-reduce.7.cloned.1.call-start = ((), (), s32[]{:S(2)}) async-start(), calls=%async_computation.3 | async-start | bytes 10485760 | tf_op jit(solution)/shard_map/psum | solution.py:121
  415.8 3.0 copy-start.10
  415.8 3.8 copy-start.9
Sparse Core Ops, SparseCore 0:
  13.4 48.7 all-gather.2
  64.3 44.7 all-gather.4
  129.8 91.2 all-reduce.4
  223.6 189.2 all-reduce.6
